TPU v7x, 128 devices: a whole 4x4x4 slice. The times are simulated.
128 devices in a mesh: group: 4 (over y), dom: 32 (over x, z, core).
Axes of the slice: x: 4, y: 4, z: 4, core: 2. Of those that a mesh axis runs over, the one named last changes fastest.
Arguments:
- mode_shapes: float32 [96, 262144], P(None, ('group', 'dom')), may hold values from -6 to 6
- send_nodes: int32 [128, 4096], P(('group', 'dom')), may hold values from 0 to 2047, as said below
- interp_index: int32 [8, 64, 16384], P(None, 'group', 'dom'), may hold values from -1 to 4095, as said below
- interp_weight: float32 [8, 64, 16384], P(None, 'group', 'dom'), may hold values from 0.1 to 1
- blend: float32 [64, 16384], P('group', 'dom'), may hold values from 0.2 to 1
- motion_gain: float32 [30, 64, 16384], P(None, 'group', 'dom'), may hold values from -3 to 3
- frequency: float32 [32], replicated, may hold values from 0.3 to 3
- volume: float32 [64, 16384], P('group', 'dom'), may hold values from 0.5 to 2
- jacobian: float32 [125, 64, 16384], P(None, 'group', 'dom'), may hold values from -1.2 to 1.2
- state: bfloat16 [320, 64, 16384], P(None, 'group', 'dom'), may hold values from -6 to 6
Outputs:
- mesh_motion: float32 [96, 64, 16384], P(None, 'group', 'dom')
- residual: float32 [320, 64, 16384], P(None, 'group', 'dom')
Inputs may be any that keep to these rules, and one draw needn't show every extreme that they name: `send_nodes`: each entry names a node local to the owner of its row, 0 to 2047. `interp_index`: A live entry is s * 32 + t, naming slot t that owner s sends to the cell's partition; a cell has 1 to 8 live entries, stored first, then -1 for padding; some cell has all 8 live. From each owner a partition uses at most 32 slots.
All inputs are finite; a program needn't handle non-finite values.
Results may differ from a plain program's by a relative error of at most 0.0003.
Values may be sent and summed in bfloat16 or wider, within the bound.
A program may use at most 192 MiB of HBM per device.

v0:
```python
import jax
import jax.numpy as jnp
from jax import lax
from jax.sharding import PartitionSpec as P

COMP = 3
VARS = 5
CASES = 32


def extended(value, sides, width):
    for axis, dim in sides:
        peers, length = (lax.axis_size(axis), value.shape[dim])
        up = [(i, (i + 1) % peers) for i in range(peers - 1)]
        down = [(j, i) for i, j in up]
        last = lax.slice_in_dim(value, length - width, length, axis=dim)
        initial = lax.slice_in_dim(value, 0, width, axis=dim)
        before = lax.ppermute(last, axis, up)
        after = lax.ppermute(initial, axis, down)
        value = jnp.concatenate([before, value, after], axis=dim)
    return value


def apply_block(block, field):
    total = jnp.zeros(field.shape, jnp.float32)
    for u in range(VARS):
        total = total + block[:, u][None, None] * field[:, :, u][:, :, None].astype(jnp.float32)
    return total


def block_length():
    return 512


def select_columns(source, picks):
    width_all, source_cols = source.shape
    pick_count = picks.shape[0]
    block_size = block_length()
    block_count = pick_count // block_size
    pick_blocks = picks.reshape(block_count, block_size)
    source_rows = jnp.arange(source_cols, dtype=jnp.int32)[:, None]

    def select_per_block(entries):
        onehot_table = jnp.where(
            source_rows == entries[None, :], jnp.float32(1.0), jnp.float32(0.0)
        )
        return jnp.dot(
            source,
            onehot_table,
            precision=lax.Precision.HIGHEST,
            preferred_element_type=jnp.float32,
        )

    picked = lax.map(select_per_block, pick_blocks)
    return picked.transpose(1, 0, 2).reshape(width_all, pick_count)


def spread_cells(arrived, safe, scaled):
    width_all, slot_cols = arrived.shape
    entry_count, row_count, col_count = safe.shape
    block_size = block_length()
    entry_blocks = safe.transpose(1, 0, 2)
    weight_blocks = scaled.transpose(1, 0, 2)
    slot_rows = jnp.arange(slot_cols, dtype=jnp.int32)[:, None]

    def spread_per_block(pair):
        entries, weights_k = pair
        onehot_table = jnp.zeros((slot_cols, block_size), jnp.float32)
        for k in range(entry_count):
            onehot_table = onehot_table + jnp.where(
                slot_rows == entries[k][None, :], weights_k[k][None, :], jnp.float32(0.0)
            )
        return jnp.dot(
            arrived,
            onehot_table,
            precision=lax.Precision.HIGHEST,
            preferred_element_type=jnp.float32,
        )

    spread = lax.map(spread_per_block, (entry_blocks, weight_blocks))
    return spread.transpose(1, 0, 2)


def local(
    mode_shapes,
    send_nodes,
    interp_index,
    interp_weight,
    blend,
    motion_gain,
    frequency,
    volume,
    jacobian,
    state,
):
    outgoing = select_columns(mode_shapes, send_nodes[0])
    arrived = lax.all_to_all(outgoing, ("group", "dom"), split_axis=1, concat_axis=1, tiled=True)
    rows = blend.shape[0]
    cols = blend.shape[1]
    live = interp_index >= 0
    safe = jnp.maximum(interp_index, 0)
    weight = jnp.where(live, interp_weight, jnp.float32(0.0))
    scaled = weight * (blend / jnp.sum(weight, axis=0))[None]
    motion = spread_cells(arrived, safe, scaled)
    gain = motion_gain.reshape(2, VARS, COMP, rows, cols)
    disp = motion.reshape(CASES, COMP, rows, cols)
    pos_force = jnp.zeros((CASES, VARS, rows, cols), jnp.float32)
    vel_force = jnp.zeros((CASES, VARS, rows, cols), jnp.float32)
    for x in range(COMP):
        pos_force = pos_force + gain[0, :, x][None] * disp[:, x][:, None]
        vel_force = vel_force + gain[1, :, x][None] * disp[:, x][:, None]
    blocks = jacobian.reshape(5, VARS, VARS, rows, cols)
    field = state.reshape(CASES, 2, VARS, rows, cols)
    omega = frequency[:, None, None, None]
    padded = extended(state, (("group", 1), ("dom", 2)), 1)
    wide = padded.reshape(CASES, 2, VARS, rows + 2, cols + 2)
    flux = apply_block(blocks[0], field)
    flux = flux + apply_block(blocks[1], wide[:, :, :, :-2, 1:-1])
    flux = flux + apply_block(blocks[2], wide[:, :, :, 2:, 1:-1])
    flux = flux + apply_block(blocks[3], wide[:, :, :, 1:-1, :-2])
    flux = flux + apply_block(blocks[4], wide[:, :, :, 1:-1, 2:])
    real_field = field[:, 0].astype(jnp.float32)
    imag_field = field[:, 1].astype(jnp.float32)
    real_part = flux[:, 0] - omega * volume[None, None] * imag_field + pos_force
    imag_part = flux[:, 1] + omega * volume[None, None] * real_field + omega * vel_force
    residual = jnp.stack([real_part, imag_part], axis=1).reshape(CASES * 2 * VARS, rows, cols)
    return (motion, residual)


def solution(mesh):
    placed = (
        P(None, ("group", "dom")),
        P(("group", "dom"), None),
        P(None, "group", "dom"),
        P(None, "group", "dom"),
        P("group", "dom"),
        P(None, "group", "dom"),
        P(),
        P("group", "dom"),
        P(None, "group", "dom"),
        P(None, "group", "dom"),
    )
    return jax.shard_map(
        local,
        mesh=mesh,
        in_specs=placed,
        out_specs=(P(None, "group", "dom"), P(None, "group", "dom")),
        check_vma=False,
    )
```

profile of v0, /device:TPU:1, one launch (start us, length us, event | category | flops | bytes accessed | tf_op | source)
XLA Modules:
  0.0 558.2 jit_solution(4023605314467550885)
XLA Ops:
  13.7 33.7 %while.23 = (s32[]{:T(128)}, f32[8,96,512]{2,1,0:T(8,128)S(1)}, s32[8,512]{1,0:T(8,128)S(1)}, f32[96,2048]{1,0:T(8,128)}, s32[]{:T(128)}) while((s32[]{:T(128)}, f32[8,96,512]{2,1,0:T(8,128)S(1)}, s32[8,512]{1,0:T(8,128)S(1)}, f32[96,2048]{1,0:T(8,128)}, s32[]{:T(128)}) %tuple.131), condition=%wide.region_2.3_spmd.clone, body=%wide.region_1.2_spmd.clone.sunk | while | flops 1210056704 | bytes 989253 | solution.py:54
  49.2 11.8 %all-to-all-start = ((f32[96,128,32]{0,2,1:T(8,128)}), f32[96,128,32]{0,2,1:T(8,128)S(1)}, u32[]{:S(2)}, u32[]{:S(2)}) async-start(f32[96,128,32]{0,2,1:T(8,128)} %bitcast.291), calls=%async_computation | async-start | bytes 4194304 | tf_op jit(solution)/shard_map/all_to_all | solution.py:97
  74.9 9.5 %copy.62 = bf16[320,16,512]{0,1,2:T(8,128)(2,1)} copy(bf16[320,16,512]{2,1,0:T(8,128)(2,1)} %param.23) | data formatting | bytes 10485760 | tf_op args[9]
  101.7 12.4 %pad_maximum_fusion.1 = bf16[320,18,514]{0,1,2:T(8,128)(2,1)} fusion(bf16[320,18,1]{0,1,2:T(8,128)(2,1)S(1)} %collective-permute-done.3, bf16[320,1,512]{0,1,2:T(2,128)(2,1)} %copy.63, bf16[320,16,512]{0,1,2:T(8,128)(2,1)} %copy.62, bf16[320,1,512]{0,1,2:T(2,128)(2,1)S(1)} %copy.61, bf16[320,18,1]{0,1,2:T(8,128)(2,1)S(1)} %collective-permute-done.2), kind=kLoop, calls=%fused_computation.74 | loop fusion | flops 29606400 | bytes 11842560 | tf_op jit(solution)/shard_map/concatenate | solution.py:20
  114.2 15.6 %copy.64 = bf16[320,18,514]{2,1,0:T(8,128)(2,1)} copy(bf16[320,18,514]{0,1,2:T(8,128)(2,1)} %pad_maximum_fusion.1) | data formatting | bytes 11842560 | tf_op jit(solution)/shard_map/concatenate | solution.py:20
  129.8 29.7 %fusion.75 = (f32[32,2,16,512]{3,2,1,0:T(8,128)}, f32[32,2,16,512]{3,2,1,0:T(8,128)}, f32[32,2,16,512]{3,2,1,0:T(8,128)}, f32[32,2,16,512]{3,2,1,0:T(8,128)}, f3...) fusion(bf16[32,2,5,18,514]{4,3,2,1,0:T(8,128)(2,1)} %bitcast.283), kind=kLoop, calls=%fused_computation.121 | loop fusion | flops 9961472 | bytes 59768832 | tf_op jit(solution)/shard_map/mul | solution.py:27
  162.7 43.4 %add_add_fusion = f32[32,2,5,16,512]{4,3,2,1,0:T(8,128)} fusion(f32[32,2,16,512]{3,2,1,0:T(8,128)} %get-tuple-element.180, f32[5,16,512]{2,1,0:T(8,128)} %get-tuple-element.242, f32[32,2,16,512]{3,2,1,0:T(8,128)} %get-tuple-element.181, f32[5,16,512]{2,1,0:T(8,128)} %get-tuple-element.243, f32[32,2,16,512]{3,2,1,0:T(8,128)} %get-tuple-element.182, ...), kind=kLoop, calls=%fused_computation.73 | loop fusion | flops 128450560 | bytes 67010560 | tf_op jit(solution)/shard_map/add | solution.py:121
  207.8 335.2 %while.24 = (s32[]{:T(128)}, f32[16,96,512]{2,0,1:T(8,128)}, s32[16,8,512]{2,1,0:T(8,128)}, f32[16,8,512]{2,1,0:T(8,128)}, f32[96,4096]{1,0:T(8,128)}, /*index=5...) while((s32[]{:T(128)}, f32[16,96,512]{2,0,1:T(8,128)}, ...), condition=%wide.region_4.5_spmd.clone.clone, body=%wide.region_3.4_spmd.clone.clone.sunk | while | flops 2464153600 | bytes 2654493 | solution.py:80
  210.1 13.6 %fusion.97 = f32[1,96,512]{2,1,0:T(8,128)S(1)} fusion(f32[96,4096]{1,0:T(8,128)} %get-tuple-element.391, f32[512]{0:T(512)S(1)} %bitcast.308, s32[512]{0:T(512)S(1)} %bitcast.316, f32[512]{0:T(512)S(1)} %bitcast.302, s32[512]{0:T(512)S(1)} %bitcast.310, f32[512]{0:T(512)S(1)} %bitcast.303, s32[512]{0:T(512)S(1)} %bitcast.311, f32[512]{0:T(512)S(1)} %bitcast.304, ...), kind=kOutput, calls=%fused_computation.54.clone.1 | convolution fusion | flops 2464153600 | bytes 1802240 | tf_op jit(solution)/shard_map/while/body/eval_jaxpr/dot_general | solution.py:73
  231.0 13.6 %fusion.97 = f32[1,96,512]{2,1,0:T(8,128)S(1)} fusion(f32[96,4096]{1,0:T(8,128)} %get-tuple-element.391, f32[512]{0:T(512)S(1)} %bitcast.308, s32[512]{0:T(512)S(1)} %bitcast.316, f32[512]{0:T(512)S(1)} %bitcast.302, s32[512]{0:T(512)S(1)} %bitcast.310, f32[512]{0:T(512)S(1)} %bitcast.303, s32[512]{0:T(512)S(1)} %bitcast.311, f32[512]{0:T(512)S(1)} %bitcast.304, ...), kind=kOutput, calls=%fused_computation.54.clone.1 | convolution fusion | flops 2464153600 | bytes 1802240 | tf_op jit(solution)/shard_map/while/body/eval_jaxpr/dot_general | solution.py:73
  251.9 13.6 %fusion.97 = f32[1,96,512]{2,1,0:T(8,128)S(1)} fusion(f32[96,4096]{1,0:T(8,128)} %get-tuple-element.391, f32[512]{0:T(512)S(1)} %bitcast.308, s32[512]{0:T(512)S(1)} %bitcast.316, f32[512]{0:T(512)S(1)} %bitcast.302, s32[512]{0:T(512)S(1)} %bitcast.310, f32[512]{0:T(512)S(1)} %bitcast.303, s32[512]{0:T(512)S(1)} %bitcast.311, f32[512]{0:T(512)S(1)} %bitcast.304, ...), kind=kOutput, calls=%fused_computation.54.clone.1 | convolution fusion | flops 2464153600 | bytes 1802240 | tf_op jit(solution)/shard_map/while/body/eval_jaxpr/dot_general | solution.py:73
  265.8 5.0 dynamic_update_slice.15
  272.9 13.6 %fusion.97 = f32[1,96,512]{2,1,0:T(8,128)S(1)} fusion(f32[96,4096]{1,0:T(8,128)} %get-tuple-element.391, f32[512]{0:T(512)S(1)} %bitcast.308, s32[512]{0:T(512)S(1)} %bitcast.316, f32[512]{0:T(512)S(1)} %bitcast.302, s32[512]{0:T(512)S(1)} %bitcast.310, f32[512]{0:T(512)S(1)} %bitcast.303, s32[512]{0:T(512)S(1)} %bitcast.311, f32[512]{0:T(512)S(1)} %bitcast.304, ...), kind=kOutput, calls=%fused_computation.54.clone.1 | convolution fusion | flops 2464153600 | bytes 1802240 | tf_op jit(solution)/shard_map/while/body/eval_jaxpr/dot_general | solution.py:73
  286.7 5.0 dynamic_update_slice.15
  293.8 13.6 %fusion.97 = f32[1,96,512]{2,1,0:T(8,128)S(1)} fusion(f32[96,4096]{1,0:T(8,128)} %get-tuple-element.391, f32[512]{0:T(512)S(1)} %bitcast.308, s32[512]{0:T(512)S(1)} %bitcast.316, f32[512]{0:T(512)S(1)} %bitcast.302, s32[512]{0:T(512)S(1)} %bitcast.310, f32[512]{0:T(512)S(1)} %bitcast.303, s32[512]{0:T(512)S(1)} %bitcast.311, f32[512]{0:T(512)S(1)} %bitcast.304, ...), kind=kOutput, calls=%fused_computation.54.clone.1 | convolution fusion | flops 2464153600 | bytes 1802240 | tf_op jit(solution)/shard_map/while/body/eval_jaxpr/dot_general | solution.py:73
  314.7 13.6 %fusion.97 = f32[1,96,512]{2,1,0:T(8,128)S(1)} fusion(f32[96,4096]{1,0:T(8,128)} %get-tuple-element.391, f32[512]{0:T(512)S(1)} %bitcast.308, s32[512]{0:T(512)S(1)} %bitcast.316, f32[512]{0:T(512)S(1)} %bitcast.302, s32[512]{0:T(512)S(1)} %bitcast.310, f32[512]{0:T(512)S(1)} %bitcast.303, s32[512]{0:T(512)S(1)} %bitcast.311, f32[512]{0:T(512)S(1)} %bitcast.304, ...), kind=kOutput, calls=%fused_computation.54.clone.1 | convolution fusion | flops 2464153600 | bytes 1802240 | tf_op jit(solution)/shard_map/while/body/eval_jaxpr/dot_general | solution.py:73
  335.6 13.6 %fusion.97 = f32[1,96,512]{2,1,0:T(8,128)S(1)} fusion(f32[96,4096]{1,0:T(8,128)} %get-tuple-element.391, f32[512]{0:T(512)S(1)} %bitcast.308, s32[512]{0:T(512)S(1)} %bitcast.316, f32[512]{0:T(512)S(1)} %bitcast.302, s32[512]{0:T(512)S(1)} %bitcast.310, f32[512]{0:T(512)S(1)} %bitcast.303, s32[512]{0:T(512)S(1)} %bitcast.311, f32[512]{0:T(512)S(1)} %bitcast.304, ...), kind=kOutput, calls=%fused_computation.54.clone.1 | convolution fusion | flops 2464153600 | bytes 1802240 | tf_op jit(solution)/shard_map/while/body/eval_jaxpr/dot_general | solution.py:73
  356.6 13.6 %fusion.97 = f32[1,96,512]{2,1,0:T(8,128)S(1)} fusion(f32[96,4096]{1,0:T(8,128)} %get-tuple-element.391, f32[512]{0:T(512)S(1)} %bitcast.308, s32[512]{0:T(512)S(1)} %bitcast.316, f32[512]{0:T(512)S(1)} %bitcast.302, s32[512]{0:T(512)S(1)} %bitcast.310, f32[512]{0:T(512)S(1)} %bitcast.303, s32[512]{0:T(512)S(1)} %bitcast.311, f32[512]{0:T(512)S(1)} %bitcast.304, ...), kind=kOutput, calls=%fused_computation.54.clone.1 | convolution fusion | flops 2464153600 | bytes 1802240 | tf_op jit(solution)/shard_map/while/body/eval_jaxpr/dot_general | solution.py:73
  370.4 5.0 dynamic_update_slice.15
  377.5 13.6 %fusion.97 = f32[1,96,512]{2,1,0:T(8,128)S(1)} fusion(f32[96,4096]{1,0:T(8,128)} %get-tuple-element.391, f32[512]{0:T(512)S(1)} %bitcast.308, s32[512]{0:T(512)S(1)} %bitcast.316, f32[512]{0:T(512)S(1)} %bitcast.302, s32[512]{0:T(512)S(1)} %bitcast.310, f32[512]{0:T(512)S(1)} %bitcast.303, s32[512]{0:T(512)S(1)} %bitcast.311, f32[512]{0:T(512)S(1)} %bitcast.304, ...), kind=kOutput, calls=%fused_computation.54.clone.1 | convolution fusion | flops 2464153600 | bytes 1802240 | tf_op jit(solution)/shard_map/while/body/eval_jaxpr/dot_general | solution.py:73
  391.3 5.0 dynamic_update_slice.15
  398.4 13.6 %fusion.97 = f32[1,96,512]{2,1,0:T(8,128)S(1)} fusion(f32[96,4096]{1,0:T(8,128)} %get-tuple-element.391, f32[512]{0:T(512)S(1)} %bitcast.308, s32[512]{0:T(512)S(1)} %bitcast.316, f32[512]{0:T(512)S(1)} %bitcast.302, s32[512]{0:T(512)S(1)} %bitcast.310, f32[512]{0:T(512)S(1)} %bitcast.303, s32[512]{0:T(512)S(1)} %bitcast.311, f32[512]{0:T(512)S(1)} %bitcast.304, ...), kind=kOutput, calls=%fused_computation.54.clone.1 | convolution fusion | flops 2464153600 | bytes 1802240 | tf_op jit(solution)/shard_map/while/body/eval_jaxpr/dot_general | solution.py:73
  419.3 13.6 %fusion.97 = f32[1,96,512]{2,1,0:T(8,128)S(1)} fusion(f32[96,4096]{1,0:T(8,128)} %get-tuple-element.391, f32[512]{0:T(512)S(1)} %bitcast.308, s32[512]{0:T(512)S(1)} %bitcast.316, f32[512]{0:T(512)S(1)} %bitcast.302, s32[512]{0:T(512)S(1)} %bitcast.310, f32[512]{0:T(512)S(1)} %bitcast.303, s32[512]{0:T(512)S(1)} %bitcast.311, f32[512]{0:T(512)S(1)} %bitcast.304, ...), kind=kOutput, calls=%fused_computation.54.clone.1 | convolution fusion | flops 2464153600 | bytes 1802240 | tf_op jit(solution)/shard_map/while/body/eval_jaxpr/dot_general | solution.py:73
  440.2 13.6 %fusion.97 = f32[1,96,512]{2,1,0:T(8,128)S(1)} fusion(f32[96,4096]{1,0:T(8,128)} %get-tuple-element.391, f32[512]{0:T(512)S(1)} %bitcast.308, s32[512]{0:T(512)S(1)} %bitcast.316, f32[512]{0:T(512)S(1)} %bitcast.302, s32[512]{0:T(512)S(1)} %bitcast.310, f32[512]{0:T(512)S(1)} %bitcast.303, s32[512]{0:T(512)S(1)} %bitcast.311, f32[512]{0:T(512)S(1)} %bitcast.304, ...), kind=kOutput, calls=%fused_computation.54.clone.1 | convolution fusion | flops 2464153600 | bytes 1802240 | tf_op jit(solution)/shard_map/while/body/eval_jaxpr/dot_general | solution.py:73
  454.1 5.0 dynamic_update_slice.15
  461.2 13.6 %fusion.97 = f32[1,96,512]{2,1,0:T(8,128)S(1)} fusion(f32[96,4096]{1,0:T(8,128)} %get-tuple-element.391, f32[512]{0:T(512)S(1)} %bitcast.308, s32[512]{0:T(512)S(1)} %bitcast.316, f32[512]{0:T(512)S(1)} %bitcast.302, s32[512]{0:T(512)S(1)} %bitcast.310, f32[512]{0:T(512)S(1)} %bitcast.303, s32[512]{0:T(512)S(1)} %bitcast.311, f32[512]{0:T(512)S(1)} %bitcast.304, ...), kind=kOutput, calls=%fused_computation.54.clone.1 | convolution fusion | flops 2464153600 | bytes 1802240 | tf_op jit(solution)/shard_map/while/body/eval_jaxpr/dot_general | solution.py:73
  475.0 5.0 dynamic_update_slice.15
  482.3 13.6 %fusion.97 = f32[1,96,512]{2,1,0:T(8,128)S(1)} fusion(f32[96,4096]{1,0:T(8,128)} %get-tuple-element.391, f32[512]{0:T(512)S(1)} %bitcast.308, s32[512]{0:T(512)S(1)} %bitcast.316, f32[512]{0:T(512)S(1)} %bitcast.302, s32[512]{0:T(512)S(1)} %bitcast.310, f32[512]{0:T(512)S(1)} %bitcast.303, s32[512]{0:T(512)S(1)} %bitcast.311, f32[512]{0:T(512)S(1)} %bitcast.304, ...), kind=kOutput, calls=%fused_computation.54.clone.1 | convolution fusion | flops 2464153600 | bytes 1802240 | tf_op jit(solution)/shard_map/while/body/eval_jaxpr/dot_general | solution.py:73
  503.2 13.6 %fusion.97 = f32[1,96,512]{2,1,0:T(8,128)S(1)} fusion(f32[96,4096]{1,0:T(8,128)} %get-tuple-element.391, f32[512]{0:T(512)S(1)} %bitcast.308, s32[512]{0:T(512)S(1)} %bitcast.316, f32[512]{0:T(512)S(1)} %bitcast.302, s32[512]{0:T(512)S(1)} %bitcast.310, f32[512]{0:T(512)S(1)} %bitcast.303, s32[512]{0:T(512)S(1)} %bitcast.311, f32[512]{0:T(512)S(1)} %bitcast.304, ...), kind=kOutput, calls=%fused_computation.54.clone.1 | convolution fusion | flops 2464153600 | bytes 1802240 | tf_op jit(solution)/shard_map/while/body/eval_jaxpr/dot_general | solution.py:73
  524.2 13.6 %fusion.97 = f32[1,96,512]{2,1,0:T(8,128)S(1)} fusion(f32[96,4096]{1,0:T(8,128)} %get-tuple-element.391, f32[512]{0:T(512)S(1)} %bitcast.308, s32[512]{0:T(512)S(1)} %bitcast.316, f32[512]{0:T(512)S(1)} %bitcast.302, s32[512]{0:T(512)S(1)} %bitcast.310, f32[512]{0:T(512)S(1)} %bitcast.303, s32[512]{0:T(512)S(1)} %bitcast.311, f32[512]{0:T(512)S(1)} %bitcast.304, ...), kind=kOutput, calls=%fused_computation.54.clone.1 | convolution fusion | flops 2464153600 | bytes 1802240 | tf_op jit(solution)/shard_map/while/body/eval_jaxpr/dot_general | solution.py:73
  545.2 7.6 %fusion.55 = (f32[32,1,5,16,512]{4,3,2,1,0:T(8,128)S(1)}, f32[32,1,5,16,512]{4,3,2,1,0:T(8,128)S(1)}) fusion(f32[32,2,5,16,512]{4,3,2,1,0:T(8,128)} %add_add_fusion, bf16[32,2,5,16,512]{4,3,2,1,0:T(8,128)(2,1)} %bitcast.285, f32[32,16,512]{2,1,0:T(8,128)S(1)} %get-tuple-element.213, f32[5,16,512]{2,1,0:T(8,128)S(1)} %copy-done.16, ...), kind=kLoop, calls=%fused_computation.78 | loop fusion | flops 24903680 | bytes 31391872 | tf_op jit(solution)/shard_map/add | solution.py:124
  552.9 5.4 pad_maximum_fusion
  (156 shorter events, 173.3 us)
Async XLA Ops:
  4.9 81.9 %collective-permute-start = (bf16[320,1,512]{2,0,1:T(8,128)(2,1)}, bf16[320,1,512]{2,0,1:T(8,128)(2,1)}, u32[]{:S(2)}, u32[]{:S(2)}) collective-permute-start(bf16[320,1,512]{2,0,1:T(8,128)(2,1)} %copy.67), channel_id=1, source_target_pairs={{0,32},{32,64},{64,96},{1,33},{33,65},{65,97},{2,34},{34,66},{66,9... | collective-permute-start | bytes 983048 | tf_op jit(solution)/shard_map/ppermute | solution.py:18
  10.4 78.9 %collective-permute-start.1 = (bf16[320,1,512]{2,0,1:T(8,128)(2,1)}, bf16[320,1,512]{2,0,1:T(8,128)(2,1)}, u32[]{:S(2)}, u32[]{:S(2)}) collective-permute-start(bf16[320,1,512]{2,0,1:T(8,128)(2,1)} %copy.68), channel_id=1, source_target_pairs={{32,0},{64,32},{96,64},{33,1},{65,33},{97,65},{34,2},{66,34},{98,6... | collective-permute-start | bytes 983048 | tf_op jit(solution)/shard_map/ppermute | solution.py:19
  47.3 18.7 %slice-start = ((s8[5242880]{0:T(1024)(128)(4,1)}), s8[1048576]{0:T(1024)(128)(4,1)S(1)}, s32[]{:S(2)}) async-start(s8[5242880]{0:T(1024)(128)(4,1)} %bitcast.286), calls=%async_computation.1 | async-start | bytes 2097152
  49.2 156.9 %all-to-all-start = ((f32[96,128,32]{0,2,1:T(8,128)}), f32[96,128,32]{0,2,1:T(8,128)S(1)}, u32[]{:S(2)}, u32[]{:S(2)}) async-start(f32[96,128,32]{0,2,1:T(8,128)} %bitcast.291), calls=%async_computation | async-start | bytes 4194304 | tf_op jit(solution)/shard_map/all_to_all | solution.py:97
  61.0 5.0 slice-start.1
  65.1 5.2 copy-start.4
  66.0 6.4 %copy-start.2 = (s32[8,16,512]{2,1,0:T(8,128)S(1)}, s32[8,16,512]{2,1,0:T(8,128)}, u32[]{:S(2)}) copy-start(s32[8,16,512]{2,1,0:T(8,128)} %param.16) | copy-start | bytes 786436
  66.0 6.4 %copy-start.3 = (f32[8,16,512]{2,1,0:T(8,128)S(1)}, f32[8,16,512]{2,1,0:T(8,128)}, u32[]{:S(2)}) copy-start(f32[8,16,512]{2,1,0:T(8,128)} %param.17) | copy-start | bytes 786436
  66.0 6.7 %copy-start.18 = (f32[16,512]{1,0:T(8,128)S(1)}, f32[16,512]{1,0:T(8,128)}, u32[]{:S(2)}) copy-start(f32[16,512]{1,0:T(8,128)} %param.18) | copy-start | bytes 98308
  66.0 6.7 %copy-start.19 = (f32[16,512]{1,0:T(8,128)S(1)}, f32[16,512]{1,0:T(8,128)}, u32[]{:S(2)}) copy-start(f32[16,512]{1,0:T(8,128)} %param.21) | copy-start | bytes 98308
  66.0 6.7 %copy-start.20 = (f32[32]{0:T(128)S(1)}, f32[32]{0:T(128)}, u32[]{:S(2)}) copy-start(f32[32]{0:T(128)} %param.20) | copy-start | bytes 388
  71.2 13.2 %copy-start.1 = (f32[25,16,512]{2,1,0:T(8,128)S(1)}, f32[25,16,512]{2,1,0:T(8,128)}, u32[]{:S(2)}) copy-start(f32[25,16,512]{2,1,0:T(8,128)} %get-tuple-element.210) | copy-start | bytes 2457604
  93.0 6.7 %collective-permute-start.2 = (bf16[320,18,1]{0,1,2:T(8,128)(2,1)S(1)}, bf16[320,18,1]{0,1,2:T(8,128)(2,1)S(1)}, u32[]{:S(2)}, u32[]{:S(2)}) collective-permute-start(bf16[320,18,1]{0,1,2:T(8,128)(2,1)S(1)} %get-tuple-element.198), channel_id=1, source_target_pairs={{0,1},{1,2},{2,3},{3,4},{4,5},{5,6},{6,7},{7,8},{8,9},{9,10},{10,1... | collective-permute-start | bytes 34568 | tf_op jit(solution)/shard_map/ppermute | solution.py:18
  96.7 5.1 collective-permute-start.3
  129.8 32.8 %copy-start.5 = (f32[5,16,512]{2,1,0:T(8,128)S(1)}, f32[5,16,512]{2,1,0:T(8,128)}, u32[]{:S(2)}) copy-start(f32[5,16,512]{2,1,0:T(8,128)} %get-tuple-element.232) | copy-start | bytes 491524
  129.8 32.8 %copy-start.6 = (f32[5,16,512]{2,1,0:T(8,128)S(1)}, f32[5,16,512]{2,1,0:T(8,128)}, u32[]{:S(2)}) copy-start(f32[5,16,512]{2,1,0:T(8,128)} %get-tuple-element.233) | copy-start | bytes 491524
  129.8 32.8 %copy-start.7 = (f32[5,16,512]{2,1,0:T(8,128)S(1)}, f32[5,16,512]{2,1,0:T(8,128)}, u32[]{:S(2)}) copy-start(f32[5,16,512]{2,1,0:T(8,128)} %get-tuple-element.234) | copy-start | bytes 491524
  129.8 32.8 %copy-start.8 = (f32[5,16,512]{2,1,0:T(8,128)S(1)}, f32[5,16,512]{2,1,0:T(8,128)}, u32[]{:S(2)}) copy-start(f32[5,16,512]{2,1,0:T(8,128)} %get-tuple-element.235) | copy-start | bytes 491524
  129.8 32.8 %copy-start.9 = (f32[5,16,512]{2,1,0:T(8,128)S(1)}, f32[5,16,512]{2,1,0:T(8,128)}, u32[]{:S(2)}) copy-start(f32[5,16,512]{2,1,0:T(8,128)} %get-tuple-element.251) | copy-start | bytes 491524
  129.8 32.8 %copy-start.10 = (f32[5,16,512]{2,1,0:T(8,128)S(1)}, f32[5,16,512]{2,1,0:T(8,128)}, u32[]{:S(2)}) copy-start(f32[5,16,512]{2,1,0:T(8,128)} %get-tuple-element.252) | copy-start | bytes 491524
  129.8 32.8 %copy-start.11 = (f32[5,16,512]{2,1,0:T(8,128)S(1)}, f32[5,16,512]{2,1,0:T(8,128)}, u32[]{:S(2)}) copy-start(f32[5,16,512]{2,1,0:T(8,128)} %get-tuple-element.253) | copy-start | bytes 491524
  207.7 337.4 %copy-start = (f32[32,16,512]{2,1,0:T(8,128)S(1)}, f32[32,16,512]{2,1,0:T(8,128)}, u32[]{:S(2)}) copy-start(f32[32,16,512]{2,1,0:T(8,128)} %broadcast_multiply_fusion) | copy-start | bytes 3145732
  207.7 337.4 %copy-start.12 = (f32[5,16,512]{2,1,0:T(8,128)S(1)}, f32[5,16,512]{2,1,0:T(8,128)}, u32[]{:S(2)}) copy-start(f32[5,16,512]{2,1,0:T(8,128)} %get-tuple-element.215) | copy-start | bytes 491524
  207.7 337.5 %copy-start.13 = (f32[5,16,512]{2,1,0:T(8,128)S(1)}, f32[5,16,512]{2,1,0:T(8,128)}, u32[]{:S(2)}) copy-start(f32[5,16,512]{2,1,0:T(8,128)} %get-tuple-element.216) | copy-start | bytes 491524
  207.7 337.5 %copy-start.14 = (f32[5,16,512]{2,1,0:T(8,128)S(1)}, f32[5,16,512]{2,1,0:T(8,128)}, u32[]{:S(2)}) copy-start(f32[5,16,512]{2,1,0:T(8,128)} %get-tuple-element.217) | copy-start | bytes 491524
  207.8 337.5 %copy-start.15 = (f32[5,16,512]{2,1,0:T(8,128)S(1)}, f32[5,16,512]{2,1,0:T(8,128)}, u32[]{:S(2)}) copy-start(f32[5,16,512]{2,1,0:T(8,128)} %get-tuple-element.218) | copy-start | bytes 491524
  207.8 337.5 %copy-start.16 = (f32[5,16,512]{2,1,0:T(8,128)S(1)}, f32[5,16,512]{2,1,0:T(8,128)}, u32[]{:S(2)}) copy-start(f32[5,16,512]{2,1,0:T(8,128)} %get-tuple-element.219) | copy-start | bytes 491524
  207.8 337.5 %copy-start.17 = (f32[5,16,512]{2,1,0:T(8,128)S(1)}, f32[5,16,512]{2,1,0:T(8,128)}, u32[]{:S(2)}) copy-start(f32[5,16,512]{2,1,0:T(8,128)} %get-tuple-element.220) | copy-start | bytes 491524
where the time goes:
time: 564 us; the launch traced here: 558 us
  matrix products  251 us (45%)
  local copies, waits for them, and re-layouts  168 us (30%)
  other arithmetic  111 us (20%)
  starting transfers between devices  23.6 us (4%)
    dot_general x16, matrix products, spread_per_block(): jnp.dot(arrived, onehot_table, precision=lax.Precision.HIGHEST, preferred...  218 us
    dynamic_update_slice x32, local copies, waits for them, and re-layouts, spread_cells(): spread = lax.map(spread_per_block, (entry_blocks, weight_blocks))  83.8 us
    add x1, other arithmetic, local(): flux = flux + apply_block(blocks[4], wide[:, :, :, 1:-1, 2:])  43.4 us
    mul x3, other arithmetic, apply_block(): block[:, u][None, None] * field[:, :, u][:, :, None].astype(jnp.float32)  37 us
    dot_general x8, matrix products, select_per_block(): jnp.dot(source, onehot_table, precision=lax.Precision.HIGHEST, preferred_...  33.4 us
    slice x16, local copies, waits for them, and re-layouts, spread_per_block(): entries[k][None, :]  16.9 us
    slice x16, local copies, waits for them, and re-layouts, spread_per_block(): weights_k[k][None, :]  16.4 us
    concatenate x1, local copies, waits for them, and re-layouts, extended(): value = jnp.concatenate([before, value, after], axis=dim)  15.6 us
  transfers between devices with their start and end apart: 5, of which 1 were waited for; matrix products, arithmetic and copies ran while one was open for 31% of the time, Pallas kernels for 0%

commit v1 on v0

v1 whole, which is shorter than its diff:
```python
import functools

import jax
import jax.numpy as jnp
from jax import lax
from jax.experimental import pallas as pl
from jax.experimental.pallas import tpu as pltpu
from jax.sharding import PartitionSpec as P

COMP = 3
VARS = 5
CASES = 32
KST = 8
SLOT = 32
BI = 16
BJ = 512
LANES = 128
ROWS = CASES * 2 * VARS
TILES = BJ // LANES
HALO_ROWS = 32
CASE_ROWS = 2 * VARS
CG = 4
R2 = CG * CASE_ROWS
PITCH = 32
RPITCH = (TILES + 2) * PITCH


def halo_kernel(st_ref, first_ref, last_ref, left_ref, right_ref, scr):
    n = HALO_ROWS * BI
    for t in range(TILES):
        tile = st_ref[:, :, t * LANES:(t + 1) * LANES].astype(jnp.float32)
        scr[t] = tile.reshape(n, LANES)
    for t in range(TILES):
        lanes = slice(t * LANES, (t + 1) * LANES)
        top = scr.at[t][pl.ds(0, HALO_ROWS, stride=BI), :]
        bottom = scr.at[t][pl.ds(BI - 1, HALO_ROWS, stride=BI), :]
        first_ref[:, lanes] = top.astype(jnp.bfloat16)
        last_ref[:, lanes] = bottom.astype(jnp.bfloat16)
    lane = lax.broadcasted_iota(jnp.int32, (16, LANES), 1)
    dims = (((1,), (1,)), ((), ()))
    pick = jnp.where(lane == 0, 1.0, 0.0).astype(jnp.bfloat16)
    edge = st_ref[:, :, 0:LANES].reshape(n, LANES)
    left_ref[...] = lax.dot_general(pick, edge, dims, preferred_element_type=jnp.float32)[0:1]
    pick = jnp.where(lane == LANES - 1, 1.0, 0.0).astype(jnp.bfloat16)
    edge = st_ref[:, :, BJ - LANES:BJ].reshape(n, LANES)
    right_ref[...] = lax.dot_general(pick, edge, dims, preferred_element_type=jnp.float32)[0:1]


def halo_strips(state):
    steps = ROWS // HALO_ROWS
    return pl.pallas_call(
        halo_kernel,
        grid=(steps,),
        in_specs=[pl.BlockSpec((HALO_ROWS, BI, BJ), lambda i: (i, 0, 0))],
        out_specs=[
            pl.BlockSpec((HALO_ROWS, BJ), lambda i: (i, 0)),
            pl.BlockSpec((HALO_ROWS, BJ), lambda i: (i, 0)),
            pl.BlockSpec((1, HALO_ROWS * BI), lambda i: (0, i)),
            pl.BlockSpec((1, HALO_ROWS * BI), lambda i: (0, i)),
        ],
        out_shape=[
            jax.ShapeDtypeStruct((ROWS, BJ), jnp.bfloat16),
            jax.ShapeDtypeStruct((ROWS, BJ), jnp.bfloat16),
            jax.ShapeDtypeStruct((1, ROWS * BI), jnp.float32),
            jax.ShapeDtypeStruct((1, ROWS * BI), jnp.float32),
        ],
        scratch_shapes=[pltpu.VMEM((TILES, HALO_ROWS * BI, LANES), jnp.float32)],
        cost_estimate=pl.CostEstimate(flops=4_000_000, bytes_accessed=6_000_000, transcendentals=0),
        name="halo_strips",
    )(state)


def merge_rows(table_ref, entries, sub):
    total = None
    for m, entry in enumerate(entries):
        row = table_ref[pl.ds(entry, 8, stride=0), :]
        total = row if total is None else jnp.where(sub == m, row, total)
    return total


def pick_kernel(nodes_ref, ms_ref, out_ref, tab, *, count):
    nodes = ms_ref.shape[1]
    for b in range(nodes // LANES):
        block = ms_ref[:, b * LANES:(b + 1) * LANES]
        padded = jnp.concatenate([block, jnp.zeros((LANES - CASES * COMP, LANES), jnp.float32)], axis=0)
        tab[b * LANES:(b + 1) * LANES, :] = padded.T
    sub = lax.broadcasted_iota(jnp.int32, (8, LANES), 0)

    @pl.loop(0, count // 32)
    def _(b):
        for g in range(4):
            entries = [nodes_ref[b * 32 + g * 8 + m] for m in range(8)]
            out_ref[b, g * 8:(g + 1) * 8, :] = merge_rows(tab, entries, sub)


def picked_rows(mode_shapes, send_nodes):
    count = send_nodes.shape[1]
    nodes = mode_shapes.shape[1]
    return pl.pallas_call(
        functools.partial(pick_kernel, count=count),
        in_specs=[pl.BlockSpec(memory_space=pltpu.SMEM), pl.BlockSpec(memory_space=pltpu.VMEM)],
        out_specs=pl.BlockSpec(memory_space=pltpu.VMEM),
        out_shape=jax.ShapeDtypeStruct((count // SLOT, SLOT, LANES), jnp.float32),
        scratch_shapes=[pltpu.VMEM((nodes, LANES), jnp.float32)],
        cost_estimate=pl.CostEstimate(flops=1_000_000, bytes_accessed=3_000_000, transcendentals=0),
        name="picked_rows",
    )(send_nodes.reshape(count), mode_shapes)


def flux_kernel(freq_ref, st_ref, up_ref, dn_ref, lf_ref, rt_ref, vol_ref, jac_ref, out_ref, q):
    step = pl.program_id(0)
    lane8 = lax.broadcasted_iota(jnp.int32, (8, LANES), 1)
    row8 = lax.broadcasted_iota(jnp.int32, (8, LANES), 0)
    dims = (((0,), (0,)), ((), ()))

    def outer(ref, at):
        values = jnp.broadcast_to(ref[...], (8, R2 * BI))
        spot = jnp.where((row8 == 0) & (lane8 == at), 1.0, 0.0)
        return lax.dot_general(values.astype(jnp.bfloat16), spot.astype(jnp.bfloat16), dims, preferred_element_type=jnp.float32)

    left = outer(lf_ref, LANES - 1)
    right = outer(rt_ref, 0)
    for r in range(R2):
        q[r * RPITCH + 8:r * RPITCH + 8 + BI, :] = left[r * BI:(r + 1) * BI]
        base = r * RPITCH + (TILES + 1) * PITCH + 8
        q[base:base + BI, :] = right[r * BI:(r + 1) * BI]
        for t in range(TILES):
            base = r * RPITCH + (t + 1) * PITCH + 8
            q[base:base + BI, :] = st_ref[r, :, t * LANES:(t + 1) * LANES].astype(jnp.float32)
    for t in range(TILES):
        lanes = slice(t * LANES, (t + 1) * LANES)
        base = (t + 1) * PITCH
        q[pl.ds(base + 7, R2, stride=RPITCH), :] = up_ref[:, lanes].astype(jnp.float32)
        q[pl.ds(base + 8 + BI, R2, stride=RPITCH), :] = dn_ref[:, lanes].astype(jnp.float32)

    first_lane = lane8 == 0
    last_lane = lane8 == LANES - 1

    @pl.loop(0, 2 * TILES * (CG // 2))
    def _(it):
        pair = it // (2 * TILES)
        pos = it % (2 * TILES)
        ti = pos // TILES
        tj = pos % TILES
        irows = pl.ds(pl.multiple_of(ti * 8, 8), 8)
        jlanes = pl.ds(pl.multiple_of(tj * LANES, LANES), LANES)
        base = pair * (2 * CASE_ROWS * RPITCH) + (tj + 1) * PITCH + 8 + ti * 8
        sets = [(cs, part) for cs in range(2) for part in range(2)]
        acc = [[None] * VARS for _ in sets]
        centers = {}

        def load(index, u, shift):
            r = index * VARS + u
            return q[pl.ds(base + r * RPITCH + shift, 8), :]

        for u in range(VARS):
            for b in range(5):
                values = []
                for index in range(4):
                    if b == 0:
                        x = load(index, u, 0)
                    elif b == 1:
                        x = load(index, u, -1)
                    elif b == 2:
                        x = load(index, u, 1)
                    elif b == 3:
                        here = pltpu.roll(load(index, u, 0), 1, 1)
                        x = jnp.where(first_lane, pltpu.roll(load(index, u, -PITCH), 1, 1), here)
                    else:
                        here = pltpu.roll(load(index, u, 0), LANES - 1, 1)
                        x = jnp.where(last_lane, pltpu.roll(load(index, u, PITCH), LANES - 1, 1), here)
                    values.append(x)
                for v in range(VARS):
                    block = jac_ref[b * VARS * VARS + v * VARS + u, irows, jlanes]
                    for index in range(4):
                        term = block * values[index]
                        old = acc[index][v]
                        acc[index][v] = term if old is None else old + term
        volume = vol_ref[irows, jlanes]
        for cs in range(2):
            scale = volume * freq_ref[step * CG + pair * 2 + cs]
            for v in range(VARS):
                real = load(cs * 2, v, 0)
                imag = load(cs * 2 + 1, v, 0)
                row = (pair * 2 + cs) * CASE_ROWS + v
                out_ref[row, irows, jlanes] = acc[cs * 2][v] - scale * imag
                out_ref[row + VARS, irows, jlanes] = acc[cs * 2 + 1][v] + scale * real


def flux_part(frequency, state, up, down, left, right, volume, jacobian):
    steps = CASES // CG
    whole = lambda i: (0, 0)
    return pl.pallas_call(
        flux_kernel,
        grid=(steps,),
        in_specs=[
            pl.BlockSpec(memory_space=pltpu.SMEM),
            pl.BlockSpec((R2, BI, BJ), lambda i: (i, 0, 0)),
            pl.BlockSpec((R2, BJ), lambda i: (i, 0)),
            pl.BlockSpec((R2, BJ), lambda i: (i, 0)),
            pl.BlockSpec((1, R2 * BI), lambda i: (0, i)),
            pl.BlockSpec((1, R2 * BI), lambda i: (0, i)),
            pl.BlockSpec((BI, BJ), whole),
            pl.BlockSpec((5 * VARS * VARS, BI, BJ), lambda i: (0, 0, 0)),
        ],
        out_specs=pl.BlockSpec((R2, BI, BJ), lambda i: (i, 0, 0)),
        out_shape=jax.ShapeDtypeStruct((ROWS, BI, BJ), jnp.float32),
        scratch_shapes=[pltpu.VMEM((R2 * RPITCH, LANES), jnp.float32)],
        cost_estimate=pl.CostEstimate(flops=140_000_000, bytes_accessed=20_000_000, transcendentals=0),
        name="flux_part",
    )(frequency, state, up, down, left, right, volume, jacobian)


def spread_kernel(freq_ref, entry_ref, index_ref, weight_ref, blend_ref, gain_ref, table_ref, flux_ref, motion_ref, out_ref, wsc, wt, acc, disp):
    total = jnp.zeros((8, LANES), jnp.float32)
    for k in range(KST):
        total = total + jnp.where(index_ref[k] >= 0, weight_ref[k], 0.0)
    ratio = blend_ref[...] / total
    for k in range(KST):
        wsc[k * 8:(k + 1) * 8, :] = jnp.where(index_ref[k] >= 0, weight_ref[k], 0.0) * ratio
    sub = lax.broadcasted_iota(jnp.int32, (8, LANES), 0)

    @pl.loop(0, 8)
    def _(s):
        mine = wsc[pl.ds(s, KST, stride=8), :]
        wide = jnp.concatenate([mine, jnp.zeros((LANES - KST, LANES), jnp.float32)], axis=0)
        wt[...] = wide.T

        @pl.loop(0, LANES // 8)
        def _(jb):
            rows = pl.ds(pl.multiple_of(jb * 8, 8), 8)
            wide8 = wt[rows, :]
            sums = None
            for k in range(KST):
                entries = [entry_ref[0, k * 8 + s, jb * 8 + m] for m in range(8)]
                value = merge_rows(table_ref, entries, sub) * jnp.broadcast_to(wide8[:, k:k + 1], (8, LANES))
                sums = value if sums is None else sums + value
            acc[rows, :] = sums

        turned = acc[...].T
        for g in range(CASES * COMP // 8):
            disp[pl.ds(g * 64 + s, 8, stride=8), :] = turned[g * 8:(g + 1) * 8]

    gains = [gain_ref[i] for i in range(2 * VARS * COMP)]

    @pl.loop(0, CASES)
    def _(c):
        freq = freq_ref[c]
        parts = [disp[pl.ds(pl.multiple_of((c * COMP + x) * 8, 8), 8), :] for x in range(COMP)]
        for x in range(COMP):
            motion_ref[c * COMP + x] = parts[x]
        for v in range(VARS):
            pos = gains[v * COMP] * parts[0]
            vel = gains[(VARS + v) * COMP] * parts[0]
            for x in range(1, COMP):
                pos = pos + gains[v * COMP + x] * parts[x]
                vel = vel + gains[(VARS + v) * COMP + x] * parts[x]
            row = c * CASE_ROWS + v
            out_ref[row] = flux_ref[row] + pos
            out_ref[row + VARS] = flux_ref[row + VARS] + freq * vel


def spread_cells(frequency, entries, index, weight, blend, gain, table, flux):
    place = lambda i: (0, i // TILES, i % TILES)
    flat = lambda i: (i // TILES, i % TILES)
    return pl.pallas_call(
        spread_kernel,
        grid=(2 * TILES,),
        in_specs=[
            pl.BlockSpec(memory_space=pltpu.SMEM),
            pl.BlockSpec((1, KST * 8, LANES), lambda i: (i, 0, 0), memory_space=pltpu.SMEM),
            pl.BlockSpec((KST, 8, LANES), place),
            pl.BlockSpec((KST, 8, LANES), place),
            pl.BlockSpec((8, LANES), flat),
            pl.BlockSpec((2 * VARS * COMP, 8, LANES), place),
            pl.BlockSpec(table.shape, lambda i: (0, 0)),
            pl.BlockSpec((ROWS, 8, LANES), place),
        ],
        out_specs=[
            pl.BlockSpec((CASES * COMP, 8, LANES), place),
            pl.BlockSpec((ROWS, 8, LANES), place),
        ],
        out_shape=[
            jax.ShapeDtypeStruct((CASES * COMP, BI, BJ), jnp.float32),
            jax.ShapeDtypeStruct((ROWS, BI, BJ), jnp.float32),
        ],
        scratch_shapes=[
            pltpu.VMEM((KST * 8, LANES), jnp.float32),
            pltpu.VMEM((LANES, LANES), jnp.float32),
            pltpu.VMEM((LANES, LANES), jnp.float32),
            pltpu.VMEM((CASES * COMP * 8, LANES), jnp.float32),
        ],
        cost_estimate=pl.CostEstimate(flops=40_000_000, bytes_accessed=28_000_000, transcendentals=0),
        name="spread_cells",
    )(frequency, entries, index, weight, blend, gain, table, flux)


def shifted(value, axis, up):
    peers = lax.axis_size(axis)
    pairs = [(i, i + 1) for i in range(peers - 1)]
    return lax.ppermute(value, axis, pairs if up else [(j, i) for i, j in pairs])


def local(mode_shapes, send_nodes, interp_index, interp_weight, blend, motion_gain, frequency, volume, jacobian, state):
    first, last, left_col, right_col = halo_strips(state)
    up = shifted(last, "group", True)
    down = shifted(first, "group", False)
    left = shifted(right_col, "dom", True)
    right = shifted(left_col, "dom", False)
    outgoing = picked_rows(mode_shapes, send_nodes)
    arrived = lax.all_to_all(outgoing, ("group", "dom"), split_axis=0, concat_axis=0, tiled=True)
    table = arrived.reshape(-1, LANES)
    safe = jnp.maximum(interp_index, 0)
    entries = safe.reshape(KST, 2, 8, TILES, LANES).transpose(1, 3, 0, 2, 4).reshape(2 * TILES, KST * 8, LANES)
    flux = flux_part(frequency, state, up, down, left, right, volume, jacobian)
    return tuple(spread_cells(frequency, entries, interp_index, interp_weight, blend, motion_gain, table, flux))


def solution(mesh):
    placed = (
        P(None, ("group", "dom")),
        P(("group", "dom"), None),
        P(None, "group", "dom"),
        P(None, "group", "dom"),
        P("group", "dom"),
        P(None, "group", "dom"),
        P(),
        P("group", "dom"),
        P(None, "group", "dom"),
        P(None, "group", "dom"),
    )
    return jax.shard_map(
        local,
        mesh=mesh,
        in_specs=placed,
        out_specs=(P(None, "group", "dom"), P(None, "group", "dom")),
        check_vma=False,
    )
```

time: 564 us -> 248 us (0.44)
  matrix products: 251 us -> 0 us
  Pallas kernels: 0 us -> 210 us
  local copies, waits for them, and re-layouts: 168 us -> 2.77 us
  other arithmetic: 111 us -> 0.03 us
  waiting for transfers between devices: 2.08 us -> 12.2 us
    dot_general x24 -> x0, matrix products: 251 us -> none  [the longest x16 218 us: spread_per_block(): jnp.dot(arrived, onehot_table, precision=lax.Precision.HIGHEST, preferred...]
    pallas_call x0 -> x4, Pallas kernels: none -> 210 us  [the longest x1 161 us: spread_cells(): pl.pallas_call(spread_kernel, grid=(2 * TILES,), in_specs=[pl.BlockSpec(m...]
    dynamic_update_slice x32 -> x0, local copies, waits for them, and re-layouts: 83.8 us -> none  [spread_cells(): spread = lax.map(spread_per_block, (entry_blocks, weight_blocks))]
    add x2 -> x0, other arithmetic: 51 us -> none  [the longest x1 43.4 us: local(): flux = flux + apply_block(blocks[4], wide[:, :, :, 1:-1, 2:])]
    slice x34 -> x0, local copies, waits for them, and re-layouts: 40.8 us -> none  [the longest x16 16.9 us: spread_per_block(): entries[k][None, :]]
    mul x4 -> x0, other arithmetic: 38.1 us -> none  [the longest x3 37 us: apply_block(): block[:, u][None, None] * field[:, :, u][:, :, None].astype(jnp.float32)]
    concatenate x1 -> x0, local copies, waits for them, and re-layouts: 15.6 us -> none  [extended(): value = jnp.concatenate([before, value, after], axis=dim)]
    concatenate x1 -> x0, other arithmetic: 12.4 us -> none  [extended(): value = jnp.concatenate([before, value, after], axis=dim)]
  transfers between devices with their start and end apart: 5 -> 5, of which waited for: 1 -> 4; matrix products, arithmetic and copies ran while one was open for 31% -> 0% of each run, Pallas kernels for 0% -> 17%
where the time goes in v1:
time: 248 us
  Pallas kernels  210 us (85%)
  starting transfers between devices  21.8 us (9%)
  waiting for transfers between devices  12.2 us (5%)
  local copies, waits for them, and re-layouts  2.77 us (1%)
    pallas_call x1, Pallas kernels, spread_cells(): pl.pallas_call(spread_kernel, grid=(2 * TILES,), in_specs=[pl.BlockSpec(m...  161 us
    pallas_call x1, Pallas kernels, flux_part(): pl.pallas_call(flux_kernel, grid=(steps,), in_specs=[pl.BlockSpec(memory_...  35.4 us
    ppermute x4, waiting for transfers between devices, shifted(): lax.ppermute(value, axis, pairs if up else [(j, i) for i, j in pairs])  12.2 us
    all_to_all x1, starting transfers between devices, local(): lax.all_to_all(outgoing, ('group', 'dom'), split_axis=0, concat_axis=0, t...  11.5 us
    ppermute x4, starting transfers between devices, shifted(): lax.ppermute(value, axis, pairs if up else [(j, i) for i, j in pairs])  10.3 us
    pallas_call x1, Pallas kernels, halo_strips(): pl.pallas_call(halo_kernel, grid=(steps,), in_specs=[pl.BlockSpec((HALO_R...  7.57 us
    pallas_call x1, Pallas kernels, picked_rows(): pl.pallas_call(functools.partial(pick_kernel, count=count), in_specs=[pl....  6.57 us
  transfers between devices with their start and end apart: 5, of which 4 were waited for; matrix products, arithmetic and copies ran while one was open for 0% of the time, Pallas kernels for 17%

profile of v1, /device:TPU:1, one launch (start us, length us, event | category | flops | bytes accessed | tf_op | source)
XLA Modules:
  0.0 247.7 jit_solution(9950115358882536992)
XLA Ops:
  0.6 6.6 %picked_rows.1 = f32[128,32,128]{2,1,0:T(8,128)} custom-call(s32[4096]{0:T(1024)} %bitcast.9, f32[96,2048]{1,0:T(8,128)} %ms_ref.1), custom_call_target="tpu_custom_call" | custom-call | flops 1000000 | bytes 3000000 | tf_op jit(solution)/shard_map/picked_rows/pallas_call | solution.py:99
  7.2 0.0 copy-start.1
  7.2 11.5 %all-to-all-start = ((f32[128,32,128]{2,1,0:T(8,128)}), f32[128,32,128]{2,1,0:T(8,128)S(1)}, u32[]{:S(2)}, u32[]{:S(2)}) async-start(f32[128,32,128]{2,1,0:T(8,128)} %picked_rows.1), calls=%async_computation | async-start | bytes 4194304 | tf_op jit(solution)/shard_map/all_to_all | solution.py:311
  18.7 7.6 %halo_strips.1 = (bf16[320,512]{1,0:T(8,128)(2,1)}, bf16[320,512]{1,0:T(8,128)(2,1)}, f32[1,5120]{1,0:T(1,128)}, f32[1,5120]{1,0:T(1,128)}) custom-call(bf16[320,16,512]{2,1,0:T(8,128)(2,1)} %st_ref.3), custom_call_target="tpu_custom_call" | custom-call | flops 4000000 | bytes 6000000 | tf_op jit(solution)/shard_map/halo_strips/pallas_call | solution.py:51
  26.3 3.3 %collective-permute-start = (bf16[320,512]{1,0:T(8,128)(2,1)}, bf16[320,512]{1,0:T(8,128)(2,1)S(1)}, u32[]{:S(2)}, u32[]{:S(2)}) collective-permute-start(bf16[320,512]{1,0:T(8,128)(2,1)} %get-tuple-element.6), channel_id=1, source_target_pairs={{0,32},{32,64},{64,96},{1,33},{33,65},{65,97},{2,34},{34,66},{66,9... | collective-permute-start | bytes 983048 | tf_op jit(solution)/shard_map/ppermute | solution.py:301
  29.5 1.3 collective-permute-start.1
  30.8 3.8 %collective-permute-start.2 = (f32[1,5120]{1,0:T(1,128)}, f32[1,5120]{1,0:T(1,128)S(1)}, u32[]{:S(2)}, u32[]{:S(2)}) collective-permute-start(f32[1,5120]{1,0:T(1,128)} %get-tuple-element.8), channel_id=1, source_target_pairs={{0,1},{1,2},{2,3},{3,4},{4,5},{5,6},{6,7},{7,8},{8,9},{9,10},{10,1... | collective-permute-start | bytes 61448 | tf_op jit(solution)/shard_map/ppermute | solution.py:301
  34.7 1.9 collective-permute-start.3
  36.6 0.0 copy-done.1
  36.7 0.7 copy.12
  37.4 0.3 collective-permute-done.2.lf_ref
  37.6 0.0 copy-start.4
  37.6 2.8 %collective-permute-done.3.rt_ref = f32[1,5120]{1,0:T(1,128)S(1)} collective-permute-done((f32[1,5120]{1,0:T(1,128)}, f32[1,5120]{1,0:T(1,128)S(1)}, u32[]{:S(2)}, u32[]{:S(2)}) %collective-permute-start.3) | collective-permute-done | bytes 20512 | tf_op jit(solution)/shard_map/ppermute | solution.py:301
  40.4 0.0 copy-start.5
  40.4 6.6 %collective-permute-done.up_ref = bf16[320,512]{1,0:T(8,128)(2,1)S(1)} collective-permute-done((bf16[320,512]{1,0:T(8,128)(2,1)}, bf16[320,512]{1,0:T(8,128)(2,1)S(1)}, u32[]{:S(2)}, u32[]{:S(2)}) %collective-permute-start) | collective-permute-done | bytes 327712 | tf_op jit(solution)/shard_map/ppermute | solution.py:301
  47.0 0.0 copy-start.2
  47.0 2.6 %collective-permute-done.1.dn_ref = bf16[320,512]{1,0:T(8,128)(2,1)S(1)} collective-permute-done((bf16[320,512]{1,0:T(8,128)(2,1)}, bf16[320,512]{1,0:T(8,128)(2,1)S(1)}, u32[]{:S(2)}, u32[]{:S(2)}) %collective-permute-start.1) | collective-permute-done | bytes 327712 | tf_op jit(solution)/shard_map/ppermute | solution.py:301
  49.5 0.0 copy-done.4
  49.5 0.0 copy-done.5
  49.6 0.0 copy-done.2
  49.6 0.0 copy-start.3
  49.6 0.7 copy-done.3
  50.3 35.4 %flux_part.1.flux_ref = f32[320,16,512]{2,1,0:T(8,128)} custom-call(f32[32]{0:T(128)} %freq_ref.3, bf16[320,16,512]{2,1,0:T(8,128)(2,1)} %st_ref.3, bf16[320,512]{1,0:T(8,128)(2,1)} %copy-done.2, bf16[320,512]{1,0:T(8,128)(2,1)} %copy-done.3, f32[1,5120]{1,0:T(1,128)} %copy-done.4, f32[1,5120]{1,0:T(1,128)} %copy-done.5, f32[16,512]{1,0:T(8,128)} %vol_ref.1, ...), custom_call_target="tpu_custom_call" | custom-call | flops 140000000 | bytes 20000000 | tf_op jit(solution)/shard_map/flux_part/pallas_call | solution.py:193
  85.7 0.0 all-to-all-done
  85.7 0.0 copy-start
  85.7 1.3 copy-done
  87.0 160.7 %spread_cells.1 = (f32[96,16,512]{2,1,0:T(8,128)}, f32[320,16,512]{2,1,0:T(8,128)}) custom-call(f32[32]{0:T(128)} %freq_ref.3, s32[8,64,128]{2,1,0:T(8,128)} %bitcast.8, s32[8,16,512]{2,1,0:T(8,128)} %index_ref.1, f32[8,16,512]{2,1,0:T(8,128)} %weight_ref.1, f32[16,512]{1,0:T(8,128)} %blend_ref.1, f32[30,16,512]{2,1,0:T(8,128)} %gain_ref.1, ...), custom_call_target="tpu_custom_call" | custom-call | flops 40000000 | bytes 28000000 | tf_op jit(solution)/shard_map/spread_cells/pallas_call | solution.py:266
  (1 shorter events, 0.0 us)
Async XLA Ops:
  7.2 29.4 %copy-start.1 = (s32[8,16,512]{2,1,0:T(8,128)S(1)}, s32[8,16,512]{2,1,0:T(8,128)}, u32[]{:S(2)}) copy-start(s32[8,16,512]{2,1,0:T(8,128)} %index_ref.1) | copy-start | bytes 786436
  7.2 78.5 %all-to-all-start = ((f32[128,32,128]{2,1,0:T(8,128)}), f32[128,32,128]{2,1,0:T(8,128)S(1)}, u32[]{:S(2)}, u32[]{:S(2)}) async-start(f32[128,32,128]{2,1,0:T(8,128)} %picked_rows.1), calls=%async_computation | async-start | bytes 4194304 | tf_op jit(solution)/shard_map/all_to_all | solution.py:311
  26.3 20.7 %collective-permute-start = (bf16[320,512]{1,0:T(8,128)(2,1)}, bf16[320,512]{1,0:T(8,128)(2,1)S(1)}, u32[]{:S(2)}, u32[]{:S(2)}) collective-permute-start(bf16[320,512]{1,0:T(8,128)(2,1)} %get-tuple-element.6), channel_id=1, source_target_pairs={{0,32},{32,64},{64,96},{1,33},{33,65},{65,97},{2,34},{34,66},{66,9... | collective-permute-start | bytes 983048 | tf_op jit(solution)/shard_map/ppermute | solution.py:301
  29.5 20.0 %collective-permute-start.1 = (bf16[320,512]{1,0:T(8,128)(2,1)}, bf16[320,512]{1,0:T(8,128)(2,1)S(1)}, u32[]{:S(2)}, u32[]{:S(2)}) collective-permute-start(bf16[320,512]{1,0:T(8,128)(2,1)} %get-tuple-element.7), channel_id=1, source_target_pairs={{32,0},{64,32},{96,64},{33,1},{65,33},{97,65},{34,2},{66,34},{98,6... | collective-permute-start | bytes 983048 | tf_op jit(solution)/shard_map/ppermute | solution.py:301
  30.8 6.8 %collective-permute-start.2 = (f32[1,5120]{1,0:T(1,128)}, f32[1,5120]{1,0:T(1,128)S(1)}, u32[]{:S(2)}, u32[]{:S(2)}) collective-permute-start(f32[1,5120]{1,0:T(1,128)} %get-tuple-element.8), channel_id=1, source_target_pairs={{0,1},{1,2},{2,3},{3,4},{4,5},{5,6},{6,7},{7,8},{8,9},{9,10},{10,1... | collective-permute-start | bytes 61448 | tf_op jit(solution)/shard_map/ppermute | solution.py:301
  34.7 5.7 %collective-permute-start.3 = (f32[1,5120]{1,0:T(1,128)}, f32[1,5120]{1,0:T(1,128)S(1)}, u32[]{:S(2)}, u32[]{:S(2)}) collective-permute-start(f32[1,5120]{1,0:T(1,128)} %get-tuple-element.9), channel_id=1, source_target_pairs={{1,0},{2,1},{3,2},{4,3},{5,4},{6,5},{7,6},{8,7},{9,8},{10,9},{11,1... | collective-permute-start | bytes 61448 | tf_op jit(solution)/shard_map/ppermute | solution.py:301
  37.6 11.9 %copy-start.4 = (f32[1,5120]{1,0:T(1,128)}, f32[1,5120]{1,0:T(1,128)S(1)}, u32[]{:S(2)}) copy-start(f32[1,5120]{1,0:T(1,128)S(1)} %collective-permute-done.2.lf_ref) | copy-start | bytes 61444
  40.4 9.1 %copy-start.5 = (f32[1,5120]{1,0:T(1,128)}, f32[1,5120]{1,0:T(1,128)S(1)}, u32[]{:S(2)}) copy-start(f32[1,5120]{1,0:T(1,128)S(1)} %collective-permute-done.3.rt_ref) | copy-start | bytes 61444
  47.0 2.6 %copy-start.2 = (bf16[320,512]{1,0:T(8,128)(2,1)}, bf16[320,512]{1,0:T(8,128)(2,1)S(1)}, u32[]{:S(2)}) copy-start(bf16[320,512]{1,0:T(8,128)(2,1)S(1)} %collective-permute-done.up_ref) | copy-start | bytes 983044
  49.6 0.7 copy-start.3
  85.7 1.3 copy-start
